TPU v7x, 512 devices: a whole 4x4x16 slice. The times are simulated.
512 devices in a mesh: section: 8 (over x, z_hi), ctx: 32 (over z_lo, y), tp: 2 (over core).
Axes of the slice: x: 4, y: 4, z: 16 (z_hi: 2, z_lo: 8; z = z_hi * 8 + z_lo), core: 2. Of those that a mesh axis runs over, the one named last changes fastest.
Arguments:
- queries: bfloat16 [8, 2, 4096, 4096], P('section', None, 'ctx', 'tp'), may hold values from -48 to 48
- keyvals: bfloat16 [8, 2, 2, 4096, 512], P('section', None, None, ('ctx', 'tp')), may hold values from -4 to 4
- segments: int32 [8, 2, 4096], P('section', None, 'ctx'), may hold values from 0 to 3, never falling along the last dimension, each value on 1 to 3072 neighbouring positions
Outputs:
- handed: bfloat16 [8, 2, 4096, 4096], P('section', None, 'ctx', 'tp')
Inputs may be any that keep to these rules, and one draw needn't show every extreme that they name: `segments`: document numbers never fall along a stream; each document is at most 3072 positions long, and one is exactly that long.
All inputs are finite; a program needn't handle non-finite values.
Results may differ from a plain program's by a relative error of at most 0.0035.
Values may be sent and summed in bfloat16 or wider, within the bound.
No kernel may reach another device: no remote copies, remote signals or barrier semaphores. Data moves between devices by JAX's collectives and lax.ppermute only.
A program may use at most 128 MiB of HBM per device.

v0:
```python
import math
import jax
import jax.numpy as jnp
from jax import lax
from jax.sharding import PartitionSpec as P

HEADS = 32
KVH = 4
HD = 128


def from_behind(block, axis, distance):
    devices = range(lax.axis_size(axis))
    route = [(i - distance, i) for i in devices if i - distance in devices]
    return lax.ppermute(block, axis, route)


def attend_piece(
    carry_state, key_value, key_docs, first, query_heads, query_docs, query_pos, query_end
):
    key_count = key_value.shape[1]
    block_len = math.gcd(key_count, 512)
    scale = 1.0 / math.sqrt(HD)

    def sweep_keys(state_in):

        def one_block(step_num, state_now):
            row_max, row_sum, out_sum = state_now
            offset = step_num * block_len
            slab_piece = lax.dynamic_slice_in_dim(key_value, offset, block_len, 1)
            key_rows = slab_piece[0].reshape(block_len, -1, HD)
            value_rows = slab_piece[1].reshape(block_len, -1, HD)
            block_docs = lax.dynamic_slice_in_dim(key_docs, offset, block_len, 0)
            key_pos = offset + jnp.arange(block_len, dtype=jnp.int32)
            allowed = (query_docs[:, None] == block_docs[None, :]) & (
                key_pos[None, :] <= query_pos[:, None]
            )
            allowed = allowed[:, None, None, :]
            scores = (
                jnp.einsum(
                    "tgjd,ngd->tgjn", query_heads, key_rows, preferred_element_type=jnp.float32
                )
                * scale
            )
            scores = jnp.where(allowed, scores, -1e30)
            new_max = jnp.maximum(row_max, jnp.max(scores, axis=-1))
            exp_terms = jnp.where(allowed, jnp.exp(scores - new_max[..., None]), 0.0)
            factor = jnp.exp(row_max - new_max)
            row_sum = factor * row_sum + jnp.sum(exp_terms, axis=-1)
            weights = exp_terms.astype(jnp.bfloat16)
            out_sum = factor[..., None] * out_sum + jnp.einsum(
                "tgjn,ngd->tgjd", weights, value_rows, preferred_element_type=jnp.float32
            )
            return (new_max, row_sum, out_sum)

        return lax.fori_loop(0, key_count // block_len, one_block, state_in)

    is_live = (first < query_end) & (key_docs[key_count - 1] >= query_docs[0])
    return lax.cond(is_live, sweep_keys, lambda state_same: state_same, carry_state)


def make_fold(streams, query_list, doc_list, query_pos, query_end):

    def fold_piece(carries, shard_piece, first):
        piece_kv, piece_docs = shard_piece
        stream_num = streams[0]
        key_value = piece_kv[0]
        updated = [
            attend_piece(
                carries[0],
                key_value,
                piece_docs[0, 0],
                first,
                query_list[stream_num],
                doc_list[stream_num],
                query_pos,
                query_end,
            )
        ]
        return tuple(updated)

    return fold_piece


def local(queries, keyvals, segments):
    tokens = queries.shape[2]
    groups = HEADS // KVH
    tp_count = lax.axis_size("tp")
    local_heads = KVH // tp_count
    query_start = lax.axis_index("ctx") * tokens
    query_pos = query_start + jnp.arange(tokens, dtype=jnp.int32)
    query_end = query_start + tokens
    query_list = [
        queries[0, stream_num].reshape(tokens, local_heads, groups, HD) for stream_num in range(2)
    ]
    doc_list = [segments[0, stream_num] for stream_num in range(2)]
    head_major = lax.all_to_all(keyvals[0], "tp", split_axis=3, concat_axis=2, tiled=True)
    key_docs = segments[0][:, None, :]
    finals = []
    for stream_num in range(2):
        fold_piece = make_fold([stream_num], query_list, doc_list, query_pos, query_end)
        result = fold_piece(
            (
                (
                    jnp.full((tokens, local_heads, groups), -1e30, jnp.float32),
                    jnp.zeros((tokens, local_heads, groups), jnp.float32),
                    jnp.zeros((tokens, local_heads, groups, HD), jnp.float32),
                ),
            ),
            (
                lax.all_gather(head_major[stream_num : stream_num + 1], "ctx", axis=2, tiled=True),
                lax.all_gather(key_docs[stream_num : stream_num + 1], "ctx", axis=2, tiled=True),
            ),
            jnp.int32(0),
        )
        finals.append(result[0])
    attended = []
    for final_state in finals:
        row_max, row_sum, out_sum = final_state
        attended.append(
            (out_sum / row_sum[..., None])
            .reshape(tokens, local_heads * groups * HD)
            .astype(jnp.bfloat16)
        )
    sent_down = from_behind(attended[0], "section", 1)
    sent_up = from_behind(attended[1], "section", -1)
    section_index = lax.axis_index("section")
    section_last = lax.axis_size("section") - 1
    down_side = jnp.where(section_index == 0, attended[1], sent_down)
    up_side = jnp.where(section_index == section_last, attended[0], sent_up)
    return jnp.stack([down_side, up_side], axis=0)[None]


def solution(mesh):
    return jax.shard_map(
        local,
        mesh=mesh,
        in_specs=(
            P("section", None, "ctx", "tp"),
            P("section", None, None, ("ctx", "tp"), None),
            P("section", None, "ctx"),
        ),
        out_specs=P("section", None, "ctx", "tp"),
        check_vma=False,
    )
```

profile of v0, /device:TPU:2, one launch (start us, length us, event | category | flops | bytes accessed | tf_op | source)
XLA Modules:
  0.0 629.4 jit_solution(5232392392438107751)
XLA Ops:
  8.7 3.9 all_to_all.15
  15.4 124.5 %all_gather.14 = s32[1,1,4096]{2,1,0:T(1,128)S(1)} all-gather(s32[1,1,128]{2,1,0:T(1,128)S(1)} %get-tuple-element.558), channel_id=1, replica_groups=mesh['section'=8,'ctx'=32,'tp'=2] {'ctx'}, dimensions={2}, use_global_device_ids=true | all-gather | bytes 16896 | tf_op jit(solution)/shard_map/all_gather | solution.py:112
  142.3 105.1 %all-gather.5.cloned.1.call-done = bf16[1,2,4096,256]{3,2,1,0:T(8,128)(2,1)} async-done(((bf16[1,2,128,256]{3,2,1,0:T(8,128)(2,1)}), bf16[1,2,4096,256]{3,2,1,0:T(8,128)(2,1)}) %all-gather.5.cloned.1.call-update) | async-done | bytes 4194320 | tf_op jit(solution)/shard_map/all_gather | solution.py:111
  247.4 103.2 %conditional.3 = (f32[128,2,8]{0,2,1:T(8,128)}, f32[128,2,8,128]{0,3,2,1:T(8,128)}) conditional(s32[]{:T(128)} %convert_element_type.35, () %tuple.51, (bf16[1,2,4096,256]{3,2,1,0:T(8,128)(2,1)}, s32[1,1,4096]{2,1,0:T(1,128)S(1)}, bf16[1,2,128,2048]{3,2,1,0:T(8,128)(2,1)S(1)}, s32[1,1,128]{2,1,0:T(1,128)S(1)}, s32[128]{0:T(128)S(1)}) %tuple.126), branch_computations={%region_6.7_spmd, %region_7.12_spmd} | conditional | flops 551496192 | bytes 46542204 | solution.py:59
  247.4 6.3 %copy.48 = bf16[1,2,4096,256]{2,3,1,0:T(8,128)(2,1)} copy(bf16[1,2,4096,256]{3,2,1,0:T(8,128)(2,1)} %get-tuple-element.500) | data formatting | bytes 8388608 | tf_op jit(solution)/shard_map
  254.8 95.8 %while.35 = (s32[]{:T(128)}, f32[128,2,8]{0,2,1:T(8,128)S(1)}, f32[128,2,8]{0,2,1:T(8,128)}, f32[128,2,8,128]{0,3,2,1:T(8,128)}, s32[1,1,128]{2,1,0:T(1,128)S(1)...) while((s32[]{:T(128)}, f32[128,2,8]{0,2,1:T(8,128)S(1)}, ...), condition=%wide.region_11.11_spmd.clone, body=%wide.region_8.10_spmd.clone.sunk | while | flops 551496192 | bytes 33959156 | solution.py:56
  273.9 3.4 fusion.64
  286.1 3.4 fusion.64
  298.3 3.4 fusion.64
  310.5 3.4 fusion.64
  322.7 3.4 fusion.64
  334.9 3.4 fusion.64
  347.1 3.4 fusion.64
  352.1 11.6 %collective-permute-start = (bf16[128,2048]{1,0:T(8,128)(2,1)S(1)}, bf16[128,2048]{1,0:T(8,128)(2,1)}, u32[]{:S(2)}, u32[]{:S(2)}) collective-permute-start(bf16[128,2048]{1,0:T(8,128)(2,1)S(1)} %copy.59), channel_id=1, source_target_pairs={{0,64},{64,128},{128,192},{192,256},{256,320},{320,384},{384,448},... | collective-permute-start | bytes 1572872 | tf_op jit(solution)/shard_map/ppermute | solution.py:15
  363.7 116.3 %all_gather.12 = s32[1,1,4096]{2,1,0:T(1,128)S(1)} all-gather(s32[1,1,128]{2,1,0:T(1,128)S(1)} %get-tuple-element.557), channel_id=1, replica_groups=mesh['section'=8,'ctx'=32,'tp'=2] {'ctx'}, dimensions={2}, use_global_device_ids=true | all-gather | bytes 16896 | tf_op jit(solution)/shard_map/all_gather | solution.py:112
  481.9 14.7 %all-gather.3.cloned.1.call-done = bf16[1,2,4096,256]{3,2,1,0:T(8,128)(2,1)} async-done(((bf16[1,2,128,256]{3,2,1,0:T(8,128)(2,1)}), bf16[1,2,4096,256]{3,2,1,0:T(8,128)(2,1)}) %all-gather.3.cloned.1.call-update) | async-done | bytes 4194320 | tf_op jit(solution)/shard_map/all_gather | solution.py:111
  496.6 103.5 %conditional.2 = (f32[128,2,8]{0,2,1:T(8,128)}, f32[128,2,8,128]{0,3,2,1:T(8,128)}) conditional(s32[]{:T(128)} %convert_element_type.32, () %tuple.49, (bf16[1,2,4096,256]{3,2,1,0:T(8,128)(2,1)}, s32[1,1,4096]{2,1,0:T(1,128)S(1)}, bf16[1,2,128,2048]{3,2,1,0:T(8,128)(2,1)S(1)}, s32[1,1,128]{2,1,0:T(1,128)S(1)}, s32[128]{0:T(128)S(1)}) %tuple.127), branch_computations={%region_0.0_spmd, %region_1.6_spmd} | conditional | flops 551496192 | bytes 46542204 | solution.py:59
  496.6 6.5 %copy.44 = bf16[1,2,4096,256]{2,3,1,0:T(8,128)(2,1)} copy(bf16[1,2,4096,256]{3,2,1,0:T(8,128)(2,1)} %get-tuple-element.495) | data formatting | bytes 8388608 | tf_op jit(solution)/shard_map
  504.1 96.0 %while.34 = (s32[]{:T(128)}, f32[128,2,8]{0,2,1:T(8,128)S(1)}, f32[128,2,8]{0,2,1:T(8,128)}, f32[128,2,8,128]{0,3,2,1:T(8,128)}, s32[1,1,128]{2,1,0:T(1,128)S(1)...) while((s32[]{:T(128)}, f32[128,2,8]{0,2,1:T(8,128)S(1)}, ...), condition=%wide.region_5.5_spmd.clone, body=%wide.region_2.4_spmd.clone.sunk | while | flops 551496192 | bytes 33959156 | solution.py:56
  535.5 3.4 fusion.72
  560.0 3.4 fusion.72
  584.4 3.4 fusion.72
  601.7 5.1 collective-permute-start.1
  607.9 13.5 %collective-permute-done.1 = bf16[128,2048]{1,0:T(8,128)(2,1)S(1)} collective-permute-done((bf16[128,2048]{1,0:T(8,128)(2,1)S(1)}, bf16[128,2048]{1,0:T(8,128)(2,1)S(1)}, u32[]{:S(2)}, u32[]{:S(2)}) %collective-permute-start.1) | collective-permute-done | bytes 524320 | tf_op jit(solution)/shard_map/ppermute | solution.py:15
  (223 shorter events, 171.2 us)
Async XLA Ops:
  6.5 8.8 %copy-start.3 = (s32[1,2,128]{2,1,0:T(2,128)S(1)}, s32[1,2,128]{2,1,0:T(2,128)}, u32[]{:S(2)}) copy-start(s32[1,2,128]{2,1,0:T(2,128)} %param.13) | copy-start | bytes 3076
  6.5 240.9 %copy-start.2 = (bf16[1,2,128,2048]{3,2,1,0:T(8,128)(2,1)S(1)}, bf16[1,2,128,2048]{3,2,1,0:T(8,128)(2,1)}, u32[]{:S(2)}) copy-start(bf16[1,2,128,2048]{3,2,1,0:T(8,128)(2,1)} %param.11) | copy-start | bytes 3145732
  6.5 240.9 %all-gather.5.cloned.1.call-start = ((), (), s32[]{:S(2)}) async-start(), calls=%async_computation.2 | async-start | bytes 4325376 | tf_op jit(solution)/shard_map/all_gather | solution.py:111
  14.6 481.9 %all-gather.3.cloned.1.call-start = ((), (), s32[]{:S(2)}) async-start(), calls=%async_computation.1 | async-start | bytes 4325376 | tf_op jit(solution)/shard_map/all_gather | solution.py:111
  258.9 4.0 copy-start
  269.2 4.7 copy-start
  281.4 4.7 copy-start
  293.6 4.7 copy-start
  305.9 4.7 copy-start
  318.1 4.7 copy-start
  330.3 4.7 copy-start
  342.5 4.7 copy-start
  352.1 254.7 %collective-permute-start = (bf16[128,2048]{1,0:T(8,128)(2,1)S(1)}, bf16[128,2048]{1,0:T(8,128)(2,1)}, u32[]{:S(2)}, u32[]{:S(2)}) collective-permute-start(bf16[128,2048]{1,0:T(8,128)(2,1)S(1)} %copy.59), channel_id=1, source_target_pairs={{0,64},{64,128},{128,192},{192,256},{256,320},{320,384},{384,448},... | collective-permute-start | bytes 1572872 | tf_op jit(solution)/shard_map/ppermute | solution.py:15
  508.3 4.0 copy-start.1
  518.6 4.7 copy-start.1
  530.8 4.7 copy-start.1
  543.1 4.7 copy-start.1
  555.3 4.7 copy-start.1
  567.5 4.7 copy-start.1
  579.8 4.7 copy-start.1
  592.0 4.7 copy-start.1
  601.7 19.8 %collective-permute-start.1 = (bf16[128,2048]{1,0:T(8,128)(2,1)S(1)}, bf16[128,2048]{1,0:T(8,128)(2,1)S(1)}, u32[]{:S(2)}, u32[]{:S(2)}) collective-permute-start(bf16[128,2048]{1,0:T(8,128)(2,1)S(1)} %copy.58), channel_id=1, source_target_pairs={{64,0},{128,64},{192,128},{256,192},{320,256},{384,320},{448,384},... | collective-permute-start | bytes 1572872 | tf_op jit(solution)/shard_map/ppermute | solution.py:15
Sparse Core Ops, SparseCore 0:
  14.7 232.6 all-gather.4
  249.5 247.0 all-gather.2
where the time goes:
time: 631 us; the launch traced here: 629 us
  blocking collectives  245 us (39%)
  waiting for transfers between devices  133 us (21%)
  matrix products  96.7 us (15%)
  other arithmetic  81.3 us (13%)
  local copies, waits for them, and re-layouts  40.2 us (6%)
  starting transfers between devices  16.8 us (3%)
  between operations  16.1 us (3%)
    all_gather x2, blocking collectives, local(): lax.all_gather(key_docs[stream_num:stream_num + 1], 'ctx', axis=2, tiled=...  241 us
    all_gather x2, waiting for transfers between devices, local(): lax.all_gather(head_major[stream_num:stream_num + 1], 'ctx', axis=2, tile...  120 us
    reduce_sum x16, other arithmetic, one_block(): row_sum = factor * row_sum + jnp.sum(exp_terms, axis=-1)  53.4 us
    dot_general x16, matrix products, one_block(): jnp.einsum('tgjn,ngd->tgjd', weights, value_rows, preferred_element_type=...  52.3 us
    dot_general x16, matrix products, one_block(): jnp.einsum('tgjd,ngd->tgjn', query_heads, key_rows, preferred_element_typ...  44.4 us
    add x16, other arithmetic, one_block(): row_sum = factor * row_sum + jnp.sum(exp_terms, axis=-1)  19.6 us
    slice x16, local copies, waits for them, and re-layouts, one_block(): value_rows = slab_piece[1].reshape(block_len, -1, HD)  17.2 us
    ppermute x2, starting transfers between devices, from_behind(): return lax.ppermute(block, axis, route)  16.7 us
  transfers between devices with their start and end apart: 4, of which 3 were waited for; matrix products, arithmetic and copies ran while one was open for 34% of the time, Pallas kernels for 0%

commit v1 on v0

--- a/solution.py
+++ b/solution.py
@@ -108,7 +108,15 @@
                 ),
             ),
             (
-                lax.all_gather(head_major[stream_num : stream_num + 1], "ctx", axis=2, tiled=True),
+                jnp.concatenate(
+                    lax.all_to_all(
+                        jnp.stack([head_major[stream_num : stream_num + 1]] * lax.axis_size("ctx")),
+                        "ctx",
+                        0,
+                        0,
+                    ),
+                    axis=2,
+                ),
                 lax.all_gather(key_docs[stream_num : stream_num + 1], "ctx", axis=2, tiled=True),
             ),
             jnp.int32(0),

time: 631 us -> 848 us (1.34)
  the two profiles are of different devices: /device:TPU:2 before, /device:TPU:4 now
where the time goes in v1:
time: 848 us; the launch traced here: 846 us
  blocking collectives  367 us (43%)
  waiting for transfers between devices  200 us (24%)
  matrix products  96.8 us (11%)
  other arithmetic  81.2 us (10%)
  local copies, waits for them, and re-layouts  60.5 us (7%)
  starting transfers between devices  36.4 us (4%)
    all_gather x2, blocking collectives, local(): lax.all_gather(key_docs[stream_num:stream_num + 1], 'ctx', axis=2, tiled=...  363 us
    all_to_all x2, waiting for transfers between devices, local(): lax.all_to_all(jnp.stack([head_major[stream_num:stream_num + 1]] * lax.ax...  188 us
    reduce_sum x16, other arithmetic, one_block(): row_sum = factor * row_sum + jnp.sum(exp_terms, axis=-1)  53.3 us
    dot_general x16, matrix products, one_block(): jnp.einsum('tgjn,ngd->tgjd', weights, value_rows, preferred_element_type=...  52.2 us
    dot_general x16, matrix products, one_block(): jnp.einsum('tgjd,ngd->tgjn', query_heads, key_rows, preferred_element_typ...  44.6 us
    all_to_all x2, starting transfers between devices, local(): lax.all_to_all(jnp.stack([head_major[stream_num:stream_num + 1]] * lax.ax...  21.3 us
    add x16, other arithmetic, one_block(): row_sum = factor * row_sum + jnp.sum(exp_terms, axis=-1)  19.6 us
    slice x16, local copies, waits for them, and re-layouts, one_block(): value_rows = slab_piece[1].reshape(block_len, -1, HD)  17.2 us
  transfers between devices with their start and end apart: 4, of which 2 were waited for; matrix products, arithmetic and copies ran while one was open for 27% of the time, Pallas kernels for 0%

profile of v1, /device:TPU:4, one launch (start us, length us, event | category | flops | bytes accessed | tf_op | source)
XLA Modules:
  0.0 845.7 jit_solution(10653444338810622211)
XLA Ops:
  2.0 3.9 all_to_all.25
  10.4 15.7 %all-to-all-start.2 = ((bf16[32,1,2,128,256]{3,4,2,1,0:T(8,128)(2,1)}), bf16[32,1,2,128,256]{3,4,2,1,0:T(8,128)(2,1)}, u32[]{:S(2)}, u32[]{:S(2)}) async-start(bf16[32,1,2,128,256]{3,4,2,1,0:T(8,128)(2,1)} %stack.17), calls=%async_computation.2 | async-start | bytes 8388608 | tf_op jit(solution)/shard_map/all_to_all | solution.py:112
  26.2 188.5 %all-to-all-done.2 = bf16[32,1,2,128,256]{3,4,2,1,0:T(8,128)(2,1)} async-done(((bf16[32,1,2,128,256]{3,4,2,1,0:T(8,128)(2,1)}), bf16[32,1,2,128,256]{3,4,2,1,0:T(8,128)(2,1)}, u32[]{:S(2)}, u32[]{:S(2)}) %all-to-all-start.2) | async-done | bytes 4194336 | tf_op jit(solution)/shard_map/all_to_all | solution.py:112
  217.7 5.7 all-to-all-start.1
  223.4 228.3 %all_gather.7 = s32[1,1,4096]{2,1,0:T(1,128)S(1)} all-gather(s32[1,1,128]{2,1,0:T(1,128)S(1)} %get-tuple-element.558), channel_id=1, replica_groups=mesh['section'=8,'ctx'=32,'tp'=2] {'ctx'}, dimensions={2}, use_global_device_ids=true | all-gather | bytes 16896 | tf_op jit(solution)/shard_map/all_gather | solution.py:120
  454.2 111.0 %conditional.3 = (f32[128,2,8]{0,2,1:T(8,128)}, f32[128,2,8,128]{0,3,2,1:T(8,128)}) conditional(s32[]{:T(128)} %convert_element_type.35, () %tuple.51, (bf16[1,2,32,128,256]{3,4,1,0,2:T(8,128)(2,1)}, s32[1,1,4096]{2,1,0:T(1,128)S(1)}, bf16[1,2,128,2048]{3,2,1,0:T(8,128)(2,1)S(1)}, s32[1,1,128]{2,1,0:T(1,128)S(1)}, s32[128]{0:T(128)S(1)}) %tuple.120), branch_computations={%region_6.7_spmd, %region_7.12_spmd} | conditional | flops 551496192 | bytes 54930812 | solution.py:59
  454.2 6.8 copy.51
  461.0 7.3 squeeze_reshape.7
  469.4 95.9 %while.35 = (s32[]{:T(128)}, f32[128,2,8]{0,2,1:T(8,128)S(1)}, f32[128,2,8]{0,2,1:T(8,128)}, f32[128,2,8,128]{0,3,2,1:T(8,128)}, s32[1,1,128]{2,1,0:T(1,128)S(1)...) while((s32[]{:T(128)}, f32[128,2,8]{0,2,1:T(8,128)S(1)}, ...), condition=%wide.region_11.11_spmd.clone, body=%wide.region_8.10_spmd.clone.sunk | while | flops 551496192 | bytes 33959156 | solution.py:56
  566.8 8.2 collective-permute-start
  575.0 134.7 %all_gather.6 = s32[1,1,4096]{2,1,0:T(1,128)S(1)} all-gather(s32[1,1,128]{2,1,0:T(1,128)S(1)} %get-tuple-element.557), channel_id=1, replica_groups=mesh['section'=8,'ctx'=32,'tp'=2] {'ctx'}, dimensions={2}, use_global_device_ids=true | all-gather | bytes 16896 | tf_op jit(solution)/shard_map/all_gather | solution.py:120
  711.7 111.5 %conditional.2 = (f32[128,2,8]{0,2,1:T(8,128)}, f32[128,2,8,128]{0,3,2,1:T(8,128)}) conditional(s32[]{:T(128)} %convert_element_type.32, () %tuple.49, (bf16[1,2,32,128,256]{3,4,1,0,2:T(8,128)(2,1)}, s32[1,1,4096]{2,1,0:T(1,128)S(1)}, bf16[1,2,128,2048]{3,2,1,0:T(8,128)(2,1)S(1)}, s32[1,1,128]{2,1,0:T(1,128)S(1)}, s32[128]{0:T(128)S(1)}) %tuple.121), branch_computations={%region_0.0_spmd, %region_1.6_spmd} | conditional | flops 551496192 | bytes 54930812 | solution.py:59
  711.9 6.9 copy.46
  718.7 7.4 squeeze_reshape.6
  727.1 96.1 %while.34 = (s32[]{:T(128)}, f32[128,2,8]{0,2,1:T(8,128)S(1)}, f32[128,2,8]{0,2,1:T(8,128)}, f32[128,2,8,128]{0,3,2,1:T(8,128)}, s32[1,1,128]{2,1,0:T(1,128)S(1)...) while((s32[]{:T(128)}, f32[128,2,8]{0,2,1:T(8,128)S(1)}, ...), condition=%wide.region_5.5_spmd.clone, body=%wide.region_2.4_spmd.clone.sunk | while | flops 551496192 | bytes 33959156 | solution.py:56
  746.3 3.4 fusion.72
  758.5 3.4 fusion.72
  770.8 3.4 fusion.72
  783.0 3.4 fusion.72
  795.3 3.4 fusion.72
  807.5 3.4 fusion.72
  819.8 3.4 fusion.72
  824.8 6.9 collective-permute-start.1
  832.8 11.8 %collective-permute-done.1 = bf16[128,2048]{1,0:T(8,128)(2,1)S(1)} collective-permute-done((bf16[128,2048]{1,0:T(8,128)(2,1)S(1)}, bf16[128,2048]{1,0:T(8,128)(2,1)S(1)}, u32[]{:S(2)}, u32[]{:S(2)}) %collective-permute-start.1) | collective-permute-done | bytes 524320 | tf_op jit(solution)/shard_map/ppermute | solution.py:15
  (227 shorter events, 186.3 us)
Async XLA Ops:
  10.4 204.3 %all-to-all-start.2 = ((bf16[32,1,2,128,256]{3,4,2,1,0:T(8,128)(2,1)}), bf16[32,1,2,128,256]{3,4,2,1,0:T(8,128)(2,1)}, u32[]{:S(2)}, u32[]{:S(2)}) async-start(bf16[32,1,2,128,256]{3,4,2,1,0:T(8,128)(2,1)} %stack.17), calls=%async_computation.2 | async-start | bytes 8388608 | tf_op jit(solution)/shard_map/all_to_all | solution.py:112
  217.7 5.7 copy-start.3
  217.7 236.5 %copy-start.2 = (bf16[1,2,128,2048]{3,2,1,0:T(8,128)(2,1)S(1)}, bf16[1,2,128,2048]{3,2,1,0:T(8,128)(2,1)}, u32[]{:S(2)}) copy-start(bf16[1,2,128,2048]{3,2,1,0:T(8,128)(2,1)} %param.11) | copy-start | bytes 3145732
  217.7 494.0 %all-to-all-start.1 = ((bf16[32,1,2,128,256]{3,4,2,1,0:T(8,128)(2,1)}), bf16[32,1,2,128,256]{3,4,2,1,0:T(8,128)(2,1)}, u32[]{:S(2)}, u32[]{:S(2)}) async-start(bf16[32,1,2,128,256]{3,4,2,1,0:T(8,128)(2,1)} %stack.15), calls=%async_computation.1 | async-start | bytes 8388608 | tf_op jit(solution)/shard_map/all_to_all | solution.py:112
  473.5 4.0 copy-start
  483.8 4.7 copy-start
  496.1 4.7 copy-start
  508.3 4.7 copy-start
  520.5 4.7 copy-start
  532.7 4.7 copy-start
  544.9 4.7 copy-start
  557.1 4.7 copy-start
  566.8 264.9 %collective-permute-start = (bf16[128,2048]{1,0:T(8,128)(2,1)S(1)}, bf16[128,2048]{1,0:T(8,128)(2,1)}, u32[]{:S(2)}, u32[]{:S(2)}) collective-permute-start(bf16[128,2048]{1,0:T(8,128)(2,1)S(1)} %copy.62), channel_id=1, source_target_pairs={{0,64},{64,128},{128,192},{192,256},{256,320},{320,384},{384,448},... | collective-permute-start | bytes 1572872 | tf_op jit(solution)/shard_map/ppermute | solution.py:15
  731.3 4.0 copy-start.1
  741.6 4.7 copy-start.1
  753.9 4.7 copy-start.1
  766.1 4.7 copy-start.1
  778.4 4.7 copy-start.1
  790.6 4.7 copy-start.1
  802.9 4.7 copy-start.1
  815.1 4.7 copy-start.1
  824.8 19.8 %collective-permute-start.1 = (bf16[128,2048]{1,0:T(8,128)(2,1)S(1)}, bf16[128,2048]{1,0:T(8,128)(2,1)S(1)}, u32[]{:S(2)}, u32[]{:S(2)}) collective-permute-start(bf16[128,2048]{1,0:T(8,128)(2,1)S(1)} %copy.61), channel_id=1, source_target_pairs={{64,0},{128,64},{192,128},{256,192},{320,256},{384,320},{448,384},... | collective-permute-start | bytes 1572872 | tf_op jit(solution)/shard_map/ppermute | solution.py:15
